TPU v7x, 32 devices: a whole 2x2x4 slice. The times are simulated.
32 devices in a mesh: segment: 2 (over x), blk: 16 (over z, y, core).
Axes of the slice: x: 2, y: 2, z: 4, core: 2. Of those that a mesh axis runs over, the one named last changes fastest.
Arguments:
- pixels: bfloat16 [128, 4, 2048], P('segment', None, 'blk'), may hold values from -6 to 6
- var_group: int32 [128], P('segment'), may hold values from 0 to 7
- var_embed: bfloat16 [128, 2048], P('segment'), may hold values from -3 to 3
- group_weight: bfloat16 [8, 4, 2048], replicated, may hold values from -3 to 3
- agg_query: bfloat16 [2048], replicated, may hold values from -180 to 180
- lat_index: int32 [2048], P('blk'), may hold values from 0 to 359
- lat_table: bfloat16 [360, 2048], replicated, may hold values from -6 to 6
- norm_gain: float32 [2048], replicated, may hold values from 0.1 to 1.9
- w_query: bfloat16 [2048, 1024], P(None, 'segment'), may hold values from -9 to 9
- w_key: bfloat16 [2048, 1024], P(None, 'segment'), may hold values from -0.125 to 0.125
- w_value: bfloat16 [2048, 1024], P(None, 'segment'), may hold values from -0.125 to 0.125
- w_out: bfloat16 [1024, 2048], P('segment'), may hold values from -1.796875 to 1.796875
Outputs:
- aggregated: bfloat16 [2048, 2048], P('blk', 'segment')
- attended: bfloat16 [2048, 2048], P('blk', 'segment')
All inputs are finite; a program needn't handle non-finite values.
Results may differ from a plain program's by a relative error of at most 0.015.
The roundings to bfloat16 on the way count: a program that leaves them out, or rounds other values in their place, can miss the bound.
Values may be sent and summed in bfloat16 or wider, within the bound.
A program may use at most 64 MiB of HBM per device.

v0:
```python
import math
import jax
import jax.numpy as jnp
from jax import lax
from jax.sharding import PartitionSpec as P

HEAD_DIM = 128


def merged(part, axis, combine):
    gathered = jax.tree.map(lambda a: lax.all_gather(a, axis), part)

    def take(source):
        return jax.tree.map(lambda a: lax.dynamic_index_in_dim(a, source, 0, False), gathered)

    return lax.fori_loop(
        1, lax.axis_size(axis), lambda source, state: combine(state, take(source)), take(0)
    )


def combine_parts(first, second):
    peak = jnp.maximum(first[0], second[0])
    scale_first = jnp.exp(first[0] - peak)
    scale_second = jnp.exp(second[0] - peak)
    total = first[1] * scale_first + second[1] * scale_second
    summed = first[2] * scale_first[:, None] + second[2] * scale_second[:, None]
    return (peak, total, summed)


def on_device(
    pixels,
    var_group,
    var_embed,
    group_weight,
    agg_query,
    lat_index,
    lat_table,
    norm_gain,
    w_query,
    w_key,
    w_value,
    w_out,
):
    highest = lax.Precision.HIGHEST
    width = var_embed.shape[1]
    groups = group_weight.shape[0]
    tok_rows = pixels.shape[2]
    lat_rows = lat_table.shape[0]
    sections = lax.axis_size("segment")
    share = width // sections
    start = lax.axis_index("segment") * share
    query32 = agg_query.astype(jnp.float32)
    group32 = group_weight.astype(jnp.float32)
    embed32 = var_embed.astype(jnp.float32)
    pixel32 = pixels.astype(jnp.float32)
    proj_group = jnp.einsum("gpd,d->gp", group32, query32, precision=highest)
    onehot = (var_group[:, None] == jnp.arange(groups, dtype=jnp.int32)[None, :]).astype(
        jnp.float32
    )
    proj_var = jnp.dot(onehot, proj_group, precision=highest)
    offset = jnp.dot(embed32, query32, precision=highest)
    scores = (
        jnp.einsum("vpt,vp->vt", pixel32, proj_var, precision=highest) + offset[:, None]
    ) / math.sqrt(width)
    lat_hot = (lat_index[:, None] == jnp.arange(lat_rows, dtype=jnp.int32)[None, :]).astype(
        jnp.bfloat16
    )
    local_peak = jnp.max(scores, axis=0)
    expo = jnp.exp(scores - local_peak[None, :])
    total = jnp.sum(expo, axis=0)
    grouped = jnp.einsum("vg,vpt->gpt", onehot, expo[:, None, :] * pixel32, precision=highest)
    summed = jnp.einsum("vt,vd->td", expo, embed32, precision=highest)
    summed = summed + jnp.einsum("gpt,gpd->td", grouped, group32, precision=highest)
    local_total = total
    local_sum = summed
    peak, total, summed = merged((local_peak, local_total, local_sum), "segment", combine_parts)
    lat_part = jnp.dot(lat_hot, lat_table, preferred_element_type=jnp.float32)
    latent = summed / total[:, None] + lat_part
    center = latent - jnp.mean(latent, axis=1, keepdims=True)
    spread = jnp.mean(center * center, axis=1, keepdims=True)
    normed = (center * lax.rsqrt(spread + 1e-05) * norm_gain[None, :]).astype(jnp.bfloat16)
    latent_share = lax.dynamic_slice_in_dim(latent, start, share, 1)
    aggregated = latent_share.astype(jnp.bfloat16)
    queries = jnp.dot(normed, w_query, preferred_element_type=jnp.float32).astype(jnp.bfloat16)
    keys = jnp.dot(normed, w_key, preferred_element_type=jnp.float32).astype(jnp.bfloat16)
    values = jnp.dot(normed, w_value, preferred_element_type=jnp.float32).astype(jnp.bfloat16)
    head_count = queries.shape[1] // HEAD_DIM
    query_heads = queries.reshape(tok_rows, head_count, HEAD_DIM)
    scale = 1.0 / math.sqrt(HEAD_DIM)

    def attend(carry, key_heads, value_heads):
        running, total, accum = carry
        logits = (
            jnp.einsum("thd,rhd->thr", query_heads, key_heads, preferred_element_type=jnp.float32)
            * scale
        )
        fresh = jnp.maximum(running, jnp.max(logits, axis=2))
        shrink = jnp.exp(running - fresh)
        expo = jnp.exp(logits - fresh[:, :, None])
        total = total * shrink + jnp.sum(expo, axis=2)
        mixed = jnp.einsum(
            "thr,rhd->thd",
            expo.astype(jnp.bfloat16),
            value_heads,
            preferred_element_type=jnp.float32,
        )
        accum = accum * shrink[:, :, None] + mixed
        return (fresh, total, accum)

    start_state = (
        jnp.full((tok_rows, head_count), -1e30, jnp.float32),
        jnp.zeros((tok_rows, head_count), jnp.float32),
        jnp.zeros((tok_rows, head_count, HEAD_DIM), jnp.float32),
    )
    carry = start_state
    key_rows = lax.all_gather(keys, "blk", axis=0, tiled=True)
    value_rows = lax.all_gather(values, "blk", axis=0, tiled=True)
    rows = key_rows.shape[0]
    block = 2048
    key_blocks = key_rows.reshape(rows // block, block, head_count, HEAD_DIM)
    value_blocks = value_rows.reshape(rows // block, block, head_count, HEAD_DIM)

    def one_block(state, blocks):
        return (attend(state, blocks[0], blocks[1]), None)

    carry, unused = lax.scan(one_block, carry, (key_blocks, value_blocks))
    running, total, accum = carry
    heads_out = (
        (accum / total[:, :, None]).reshape(tok_rows, head_count * HEAD_DIM).astype(jnp.bfloat16)
    )
    partial_value = jnp.dot(heads_out, w_out, preferred_element_type=jnp.float32)
    attended = lax.psum_scatter(
        partial_value.astype(jnp.bfloat16), "segment", scatter_dimension=1, tiled=True
    )
    return (aggregated, attended)


def solution(mesh):
    in_specs = (
        P("segment", None, "blk"),
        P("segment"),
        P("segment", None),
        P(),
        P(),
        P("blk"),
        P(),
        P(),
        P(None, "segment"),
        P(None, "segment"),
        P(None, "segment"),
        P("segment", None),
    )
    out_specs = (P("blk", "segment"), P("blk", "segment"))
    return jax.shard_map(
        on_device, mesh=mesh, in_specs=in_specs, out_specs=out_specs, check_vma=False
    )
```

profile of v0, /device:TPU:0, one launch (start us, length us, event | category | flops | bytes accessed | tf_op | source)
XLA Modules:
  0.0 174.4 jit_solution(17387931946372268658)
XLA Ops:
  7.2 0.0 copy-start
  7.2 0.0 copy-start.4
  7.2 0.0 all-gather.13.cloned.1.call-start
  7.2 0.9 reshape.118
  8.1 0.7 reshape.114
  8.8 1.1 convolution_bitcast_fusion.1
  9.9 1.6 fusion.48
  11.5 0.9 fusion.32
  12.4 1.2 fusion.49
  13.6 0.1 fusion.34
  13.7 0.1 fusion.46
  13.8 0.9 convert_multiply_fusion
  14.7 0.9 fusion.27
  15.6 1.5 convolution_bitcast_fusion
  17.1 0.0 copy-done.4
  17.1 1.6 convolution_add_fusion.1
  18.8 0.0 all-gather.13.cloned.1.call-update
  18.8 0.0 all-gather.9.cloned.1.call-start
  18.8 5.2 %all-gather.4 = f32[2,1,128]{2,1,0:T(1,128)S(1)} all-gather(f32[1,1,128]{2,1,0:T(1,128)S(1)} %bitcast.113), channel_id=4, replica_groups=mesh['segment'=2,'blk'=16] {'segment'}, dimensions={0}, use_global_device_ids=true | all-gather | bytes 1536 | tf_op jit(solution)/shard_map/all_gather | solution.py:11
  24.0 4.2 %all-gather.3 = f32[2,1,128]{2,1,0:T(1,128)S(1)} all-gather(f32[1,1,128]{2,1,0:T(1,128)S(1)} %bitcast.112), channel_id=3, replica_groups=mesh['segment'=2,'blk'=16] {'segment'}, dimensions={0}, use_global_device_ids=true | all-gather | bytes 1536 | tf_op jit(solution)/shard_map/all_gather | solution.py:11
  28.2 26.5 %all-gather.13.cloned.1.call-done = f32[256,2048]{1,0:T(8,128)} async-done(((f32[128,2048]{1,0:T(8,128)}), f32[256,2048]{1,0:T(8,128)}) %all-gather.13.cloned.1.call-update) | async-done | bytes 2097168 | tf_op jit(solution)/shard_map/all_gather | solution.py:11
  54.8 0.0 copy-done.6
  54.8 2.6 %fusion.47 = (f32[128]{0:T(128)S(1)}, f32[128,2048]{1,0:T(8,128)S(1)}) fusion(bf16[360,2048]{1,0:T(8,128)(2,1)} %param.18, s32[128]{0:T(128)S(1)} %copy-done.6, f32[128]{0:T(128)S(1)} %get-tuple-element.33, f32[128]{0:T(128)S(1)} %get-tuple-element.35, f32[256,2048]{1,0:T(8,128)} %all-gather.13.cloned.1.call-done, f32[128]{0:T(128)S(1)} %get-tuple-element.34), kind=kOutput, calls=%fused_computation.65 | convolution fusion | flops 190362496 | bytes 4622848 | tf_op jit(solution)/shard_map/dot_general | solution.py:77
  57.4 0.0 copy-start.3
  57.4 0.3 multiply_reduce_fusion
  57.6 0.8 copy-done.2
  58.4 0.0 copy-done.5
  58.4 0.2 multiply_convert_fusion
  58.6 0.7 copy-done.3
  59.3 1.1 convolution_convert_fusion.3
  60.4 0.0 all-gather.9.cloned.1.call-update
  60.5 0.0 all-gather.11.cloned.1.call-start
  60.5 2.7 %convolution_convert_fusion.1 = bf16[128,512]{1,0:T(8,128)(2,1)} fusion(bf16[128,2048]{1,0:T(8,128)(2,1)S(1)} %multiply_convert_fusion, bf16[2048,512]{1,0:T(8,128)(2,1)} %param.22), kind=kOutput, calls=%fused_computation.17 | convolution fusion | flops 268500992 | bytes 2752512 | tf_op jit(solution)/shard_map/dot_general | solution.py:86
  63.2 0.0 all-gather.11.cloned.1.call-update
  63.2 0.0 reduce-scatter.2.cloned.1.call-start
  63.3 2.0 %fusion.16 = bf16[16,4,8,128]{3,2,1,0:T(8,128)(2,1)S(1)} fusion(bf16[128,2048]{1,0:T(8,128)(2,1)S(1)} %multiply_convert_fusion, bf16[2048,512]{1,0:T(8,128)(2,1)} %param.20), kind=kOutput, calls=%fused_computation.20 | convolution fusion | flops 268500992 | bytes 2752512 | tf_op jit(solution)/shard_map/dot_general | solution.py:84
  65.3 36.8 %all-gather.9.cloned.1.call-done = bf16[2048,512]{1,0:T(8,128)(2,1)} async-done(((bf16[128,512]{1,0:T(8,128)(2,1)}), bf16[2048,512]{1,0:T(8,128)(2,1)}) %all-gather.9.cloned.1.call-update) | async-done | bytes 2097168 | tf_op jit(solution)/shard_map/all_gather | solution.py:116
  102.1 2.3 %bitcast_reduce_fusion = (f32[128,4]{0,1:T(4,128)S(1)}, f32[4,2048,128]{2,1,0:T(8,128)S(1)}) fusion(bf16[16,4,8,128]{3,2,1,0:T(8,128)(2,1)S(1)} %fusion.16, bf16[2048,512]{1,0:T(8,128)(2,1)} %all-gather.9.cloned.1.call-done), kind=kOutput, calls=%fused_computation.1 | convolution fusion | flops 270532096 | bytes 6424576 | tf_op jit(solution)/shard_map/while/body/eval_jaxpr/thd,rhd->thr/dot_general | solution.py:94
  104.5 0.0 copy-start.1
  104.5 0.7 fusion.1
  105.2 1.2 copy-done.1
  106.4 38.7 %all-gather.11.cloned.1.call-done = bf16[2048,512]{1,0:T(8,128)(2,1)} async-done(((bf16[128,512]{1,0:T(8,128)(2,1)}), bf16[2048,512]{1,0:T(8,128)(2,1)}) %all-gather.11.cloned.1.call-update) | async-done | bytes 2097168 | tf_op jit(solution)/shard_map/all_gather | solution.py:117
  145.1 4.0 %copy.29 = bf16[2048,512]{0,1:T(8,128)(2,1)} copy(bf16[2048,512]{1,0:T(8,128)(2,1)} %all-gather.11.cloned.1.call-done) | data formatting | bytes 4194304 | tf_op jit(solution)/shard_map/while/body/jit(dynamic_index_in_dim)/squeeze | solution.py:126
  149.1 4.0 %fusion.20 = bf16[128,4,128]{0,2,1:T(8,128)(2,1)S(1)} fusion(bf16[2048,4,128]{0,2,1:T(8,128)(2,1)} %bitcast.108, f32[4,2048,128]{2,1,0:T(8,128)} %copy-done.1, f32[128,4]{0,1:T(4,128)S(1)} %broadcast_maximum_fusion, f32[128,4]{0,1:T(4,128)S(1)} %get-tuple-element.46, f32[128,4]{0,1:T(4,128)S(1)} %get-tuple-element.38), kind=kOutput, calls=%fused_computation.23 | convolution fusion | flops 271777792 | bytes 6428672 | tf_op jit(solution)/shard_map/while/body/eval_jaxpr/thr,rhd->thd/dot_general | solution.py:101
  153.1 1.3 convolution_convert_fusion
  154.3 0.0 reduce-scatter.2.cloned.1.call-update
  154.4 1.8 %dynamic-slice_convert_fusion = bf16[128,1024]{1,0:T(8,128)(2,1)} fusion(f32[128,2048]{1,0:T(8,128)} %copy-done.2, s32[]{:T(128)S(6)} %select_n.12), kind=kLoop, calls=%fused_computation.30 | loop fusion | bytes 524292 | tf_op jit(solution)/shard_map/convert_element_type | solution.py:83
  156.2 11.7 %reduce-scatter.2.cloned.1.call-done = bf16[128,1024]{1,0:T(8,128)(2,1)} async-done(((bf16[128,2048]{1,0:T(8,128)(2,1)}), bf16[128,1024]{1,0:T(8,128)(2,1)}) %reduce-scatter.2.cloned.1.call-update) | async-done | bytes 262160 | tf_op jit(solution)/shard_map/reduce_scatter | solution.py:132
  (9 shorter events, 0.0 us)
Async XLA Ops:
  7.2 145.9 %copy-start = (bf16[512,2048]{1,0:T(8,128)(2,1)S(1)}, bf16[512,2048]{1,0:T(8,128)(2,1)}, u32[]{:S(2)}) copy-start(bf16[512,2048]{1,0:T(8,128)(2,1)} %param.23) | copy-start | bytes 6291460
  7.2 10.0 %copy-start.4 = (bf16[64,2048]{1,0:T(8,128)(2,1)S(1)}, bf16[64,2048]{1,0:T(8,128)(2,1)}, u32[]{:S(2)}) copy-start(bf16[64,2048]{1,0:T(8,128)(2,1)} %param.14) | copy-start | bytes 786436
  7.2 47.6 %all-gather.13.cloned.1.call-start = ((), (), s32[]{:S(2)}) async-start(), calls=%async_computation.4 | async-start | bytes 3145728 | tf_op jit(solution)/shard_map/all_gather | solution.py:11
  15.6 39.2 %copy-start.6 = (s32[128]{0:T(128)S(1)}, s32[128]{0:T(128)}, u32[]{:S(2)}) copy-start(s32[128]{0:T(128)} %param.17) | copy-start | bytes 1540
  18.8 83.3 %all-gather.9.cloned.1.call-start = ((), (), s32[]{:S(2)}) async-start(), calls=%async_computation.1 | async-start | bytes 2228224 | tf_op jit(solution)/shard_map/all_gather | solution.py:116
  54.8 3.6 %copy-start.5 = (f32[2048]{0:T(1024)S(1)}, f32[2048]{0:T(1024)}, u32[]{:S(2)}) copy-start(f32[2048]{0:T(1024)} %param.19) | copy-start | bytes 24580
  57.4 1.1 copy-start.2
  57.4 2.0 %copy-start.3 = (bf16[2048,512]{1,0:T(8,128)(2,1)S(1)}, bf16[2048,512]{1,0:T(8,128)(2,1)}, u32[]{:S(2)}) copy-start(bf16[2048,512]{1,0:T(8,128)(2,1)} %param.21) | copy-start | bytes 6291460
  60.5 84.6 %all-gather.11.cloned.1.call-start = ((), (), s32[]{:S(2)}) async-start(), calls=%async_computation.2 | async-start | bytes 2228224 | tf_op jit(solution)/shard_map/all_gather | solution.py:117
  63.2 104.6 %reduce-scatter.2.cloned.1.call-start = ((), (), s32[]{:S(2)}) async-start(), calls=%async_computation.3 | async-start | bytes 786432 | tf_op jit(solution)/shard_map/reduce_scatter | solution.py:132
  104.5 1.9 %copy-start.1 = (f32[4,2048,128]{2,1,0:T(8,128)}, f32[4,2048,128]{2,1,0:T(8,128)S(1)}, u32[]{:S(2)}) copy-start(f32[4,2048,128]{2,1,0:T(8,128)S(1)} %get-tuple-element.50) | copy-start | bytes 12582916
Sparse Core Ops, SparseCore 0:
  18.9 35.8 all-gather.12
  60.6 41.4 all-gather.8
  104.9 40.1 all-gather.10
  154.5 13.3 reduce-scatter.1
where the time goes:
time: 175 us; the launch traced here: 174 us
  waiting for transfers between devices  114 us (65%)
  matrix products  24.9 us (14%)
  between operations  13.9 us (8%)
  local copies, waits for them, and re-layouts  10.1 us (6%)
  blocking collectives  9.39 us (5%)
  other arithmetic  2.26 us (1%)
    all_gather x1, waiting for transfers between devices, on_device(): value_rows = lax.all_gather(values, 'blk', axis=0, tiled=True)  38.7 us
    all_gather x1, waiting for transfers between devices, on_device(): key_rows = lax.all_gather(keys, 'blk', axis=0, tiled=True)  36.8 us
    all_gather x1, waiting for transfers between devices, merged(): gathered = jax.tree.map(lambda a: lax.all_gather(a, axis), part)  26.5 us
    reduce_scatter x1, waiting for transfers between devices, on_device(): lax.psum_scatter(partial_value.astype(jnp.bfloat16), 'segment', scatter_d...  11.7 us
    all_gather x2, blocking collectives, merged(): gathered = jax.tree.map(lambda a: lax.all_gather(a, axis), part)  9.39 us
    unnamed x16, local copies, waits for them, and re-layouts  4.29 us
    squeeze x1, local copies, waits for them, and re-layouts, on_device(): carry, unused = lax.scan(one_block, carry, (key_blocks, value_blocks))  3.99 us
    dot_general x1, matrix products, attend(): jnp.einsum('thr,rhd->thd', expo.astype(jnp.bfloat16), value_heads, prefer...  3.99 us
  transfers between devices with their start and end apart: 4, of which 4 were waited for; matrix products, arithmetic and copies ran while one was open for 5% of the time, Pallas kernels for 0%

commit v1 on v0

--- a/solution.py
+++ b/solution.py
@@ -5,6 +5,29 @@
 from jax.sharding import PartitionSpec as P
 
 HEAD_DIM = 128
+
+
+def tokens_attach(unit, dim_k):
+    t1 = list(unit.shape[1:])
+    t1[dim_k] *= unit.shape[0]
+    next_value = jnp.moveaxis(unit, 0, dim_k).reshape(t1)
+    return next_value
+
+
+def write_shapes(tile_in, dev_axis):
+    n_slots = lax.psum(1, dev_axis)
+    tile_out = tile_in[None]
+    for q in range(n_slots.bit_length() - 1):
+        e_now = 1 << q
+        lower = tuple(((dev_j, dev_j ^ e_now) for dev_j in range(n_slots)))
+        main = lax.ppermute(tile_out, dev_axis, lower)
+        local_next = jnp.stack([tile_out, main], 0)
+        all_values = lax.axis_index(dev_axis)
+        base_arr = all_values >> q & 1
+        tile_out = jnp.where(base_arr == 0, local_next, local_next[::-1]).reshape(
+            -1, *tile_in.shape
+        )
+    return tile_out
 
 
 def merged(part, axis, combine):
@@ -113,7 +136,8 @@
         jnp.zeros((tok_rows, head_count, HEAD_DIM), jnp.float32),
     )
     carry = start_state
-    key_rows = lax.all_gather(keys, "blk", axis=0, tiled=True)
+    t_next = write_shapes(keys, "blk")
+    key_rows = tokens_attach(t_next, 0)
     value_rows = lax.all_gather(values, "blk", axis=0, tiled=True)
     rows = key_rows.shape[0]
     block = 2048

time: 175 us -> 190 us (1.086)
  local copies, waits for them, and re-layouts: 10.1 us -> 16.7 us
  other arithmetic: 2.26 us -> 8.3 us
  starting transfers between devices: 0.16 us -> 5.7 us
  waiting for transfers between devices: 114 us -> 111 us
    ppermute x0 -> x4, waiting for transfers between devices: none -> 72.3 us  [write_shapes(): main = lax.ppermute(tile_out, dev_axis, lower)]
    all_gather x1, waiting for transfers between devices: 38.7 us -> 0.01 us  [on_device(): value_rows = lax.all_gather(values, 'blk', axis=0, tiled=True)]
    all_gather x1 -> x0, waiting for transfers between devices: 36.8 us -> none  [on_device(): key_rows = lax.all_gather(keys, 'blk', axis=0, tiled=True)]
    ppermute x0 -> x4, starting transfers between devices: none -> 5.58 us  [write_shapes(): main = lax.ppermute(tile_out, dev_axis, lower)]
    squeeze x1 -> x2, local copies, waits for them, and re-layouts: 3.99 us -> 8.13 us  [on_device(): carry, unused = lax.scan(one_block, carry, (key_blocks, value_blocks))]
    select_n x0 -> x3, other arithmetic: none -> 3.2 us  [write_shapes(): jnp.where(base_arr == 0, local_next, local_next[::-1])]
    another operation x0 -> x5, other arithmetic: none -> 2.84 us  [write_shapes(): local_next = jnp.stack([tile_out, main], 0)]
    select_n x0 -> x1, local copies, waits for them, and re-layouts: none -> 2.45 us  [write_shapes(): jnp.where(base_arr == 0, local_next, local_next[::-1])]
  transfers between devices with their start and end apart: 4 -> 7, of which waited for: 4 -> 6; matrix products, arithmetic and copies ran while one was open for 5% -> 12% of each run, Pallas kernels for 0% -> 0%
where the time goes in v1:
time: 190 us; the launch traced here: 189 us
  waiting for transfers between devices  111 us (58%)
  matrix products  24.4 us (13%)
  local copies, waits for them, and re-layouts  16.7 us (9%)
  between operations  13.9 us (7%)
  blocking collectives  9.38 us (5%)
  other arithmetic  8.3 us (4%)
  starting transfers between devices  5.7 us (3%)
    ppermute x4, waiting for transfers between devices, write_shapes(): main = lax.ppermute(tile_out, dev_axis, lower)  72.3 us
    all_gather x1, waiting for transfers between devices, merged(): gathered = jax.tree.map(lambda a: lax.all_gather(a, axis), part)  26.5 us
    reduce_scatter x1, waiting for transfers between devices, on_device(): lax.psum_scatter(partial_value.astype(jnp.bfloat16), 'segment', scatter_d...  12.1 us
    all_gather x2, blocking collectives, merged(): gathered = jax.tree.map(lambda a: lax.all_gather(a, axis), part)  9.38 us
    squeeze x2, local copies, waits for them, and re-layouts, on_device(): carry, unused = lax.scan(one_block, carry, (key_blocks, value_blocks))  8.13 us
    ppermute x4, starting transfers between devices, write_shapes(): main = lax.ppermute(tile_out, dev_axis, lower)  5.58 us
    unnamed x18, local copies, waits for them, and re-layouts  4.29 us
    dot_general x1, matrix products, attend(): jnp.einsum('thr,rhd->thd', expo.astype(jnp.bfloat16), value_heads, prefer...  3.98 us
  transfers between devices with their start and end apart: 7, of which 6 were waited for; matrix products, arithmetic and copies ran while one was open for 12% of the time, Pallas kernels for 0%

profile of v1, /device:TPU:0, one launch (start us, length us, event | category | flops | bytes accessed | tf_op | source)
XLA Modules:
  0.0 189.3 jit_solution(16521656248652557285)
XLA Ops:
  7.2 0.9 reshape.129
  8.1 0.7 reshape.125
  8.8 1.1 convolution_bitcast_fusion.1
  9.9 1.6 fusion.48
  11.5 0.9 fusion.33
  12.4 1.2 fusion.49
  13.6 0.1 fusion.31
  13.7 0.1 fusion.46
  13.8 0.9 convert_multiply_fusion
  14.7 0.8 fusion.28
  15.5 1.5 convolution_bitcast_fusion
  17.1 1.6 convolution_add_fusion.1
  18.7 0.0 all-gather.8.cloned.1.call-start
  18.8 5.2 %all-gather.4 = f32[2,1,128]{2,1,0:T(1,128)S(1)} all-gather(f32[1,1,128]{2,1,0:T(1,128)S(1)} %bitcast.132), channel_id=4, replica_groups=mesh['segment'=2,'blk'=16] {'segment'}, dimensions={0}, use_global_device_ids=true | all-gather | bytes 1536 | tf_op jit(solution)/shard_map/all_gather | solution.py:34
  23.9 4.2 %all-gather.3 = f32[2,1,128]{2,1,0:T(1,128)S(1)} all-gather(f32[1,1,128]{2,1,0:T(1,128)S(1)} %bitcast.131), channel_id=3, replica_groups=mesh['segment'=2,'blk'=16] {'segment'}, dimensions={0}, use_global_device_ids=true | all-gather | bytes 1536 | tf_op jit(solution)/shard_map/all_gather | solution.py:34
  28.2 26.5 %all-gather.10.cloned.1.call-done = f32[256,2048]{1,0:T(8,128)} async-done(((f32[128,2048]{1,0:T(8,128)}), f32[256,2048]{1,0:T(8,128)}) %all-gather.10.cloned.1.call-update) | async-done | bytes 2097168 | tf_op jit(solution)/shard_map/all_gather | solution.py:34
  54.7 2.6 %fusion.47 = (f32[128]{0:T(128)S(1)}, f32[128,2048]{1,0:T(8,128)S(1)}) fusion(bf16[360,2048]{1,0:T(8,128)(2,1)} %param.18, s32[128]{0:T(128)S(1)} %copy-done.7, f32[128]{0:T(128)S(1)} %get-tuple-element.33, f32[128]{0:T(128)S(1)} %get-tuple-element.35, f32[256,2048]{1,0:T(8,128)} %all-gather.10.cloned.1.call-done, f32[128]{0:T(128)S(1)} %get-tuple-element.34), kind=kOutput, calls=%fused_computation.73 | convolution fusion | flops 190362496 | bytes 4622848 | tf_op jit(solution)/shard_map/dot_general | solution.py:100
  57.3 0.3 multiply_reduce_fusion
  57.6 0.2 multiply_convert_fusion
  57.8 1.5 copy-done.4
  59.3 0.4 convolution_convert_fusion.3
  59.7 0.1 collective-permute-start
  59.8 1.3 collective-permute-done
  61.2 0.1 fusion.23
  61.2 1.5 collective-permute-start.1
  62.8 2.7 %convolution_convert_fusion.1 = bf16[128,512]{1,0:T(8,128)(2,1)} fusion(bf16[128,2048]{1,0:T(8,128)(2,1)S(1)} %multiply_convert_fusion, bf16[2048,512]{1,0:T(8,128)(2,1)} %param.22), kind=kOutput, calls=%fused_computation.17 | convolution fusion | flops 268500992 | bytes 2752512 | tf_op jit(solution)/shard_map/dot_general | solution.py:109
  65.6 4.1 %collective-permute-done.1 = bf16[2,128,512]{2,1,0:T(8,128)(2,1)S(1)} collective-permute-done((bf16[2,128,512]{2,1,0:T(8,128)(2,1)S(1)}, bf16[2,128,512]{2,1,0:T(8,128)(2,1)S(1)}, u32[]{:S(2)}, u32[]{:S(2)}) %collective-permute-start.1) | collective-permute-done | bytes 262176 | tf_op jit(solution)/shard_map/ppermute | solution.py:23
  69.7 0.1 pad_maximum_fusion.2
  69.7 0.1 reverse_select_fusion.2
  69.8 1.6 collective-permute-start.2
  71.4 16.0 %collective-permute-done.2 = bf16[4,128,512]{2,1,0:T(8,128)(2,1)} collective-permute-done((bf16[4,128,512]{2,1,0:T(8,128)(2,1)S(1)}, bf16[4,128,512]{2,1,0:T(8,128)(2,1)}, u32[]{:S(2)}, u32[]{:S(2)}) %collective-permute-start.2) | collective-permute-done | bytes 524320 | tf_op jit(solution)/shard_map/ppermute | solution.py:23
  87.3 1.1 pad_maximum_fusion.1
  88.5 1.2 reverse_select_fusion.1
  89.7 2.4 %copy.27 = bf16[2,4,128,512]{2,1,0,3:T(4,128)(2,1)} copy(bf16[2,4,128,512]{3,2,1,0:T(8,128)(2,1)} %reverse_select_fusion.1) | data formatting | bytes 2097152 | tf_op jit(solution)/shard_map/jit(_where)/select_n | solution.py:27
  92.1 2.4 %collective-permute-start.3 = (bf16[8,128,512]{1,0,2:T(8,128)(2,1)}, bf16[8,128,512]{1,0,2:T(8,128)(2,1)}, u32[]{:S(2)}, u32[]{:S(2)}) collective-permute-start(bf16[8,128,512]{1,0,2:T(8,128)(2,1)} %bitcast.117), channel_id=1, source_target_pairs={{0,8},{1,9},{2,10},{3,11},{4,12},{5,13},{6,14},{7,15},{8,0},{9,1},... | collective-permute-start | bytes 3145736 | tf_op jit(solution)/shard_map/ppermute | solution.py:23
  94.5 2.1 %fusion.13 = bf16[16,4,8,128]{3,2,1,0:T(8,128)(2,1)S(1)} fusion(bf16[128,2048]{1,0:T(8,128)(2,1)S(1)} %multiply_convert_fusion, bf16[2048,512]{1,0:T(8,128)(2,1)} %param.20), kind=kOutput, calls=%fused_computation.20 | convolution fusion | flops 268500992 | bytes 2752512 | tf_op jit(solution)/shard_map/dot_general | solution.py:107
  96.7 50.9 %collective-permute-done.3 = bf16[8,128,512]{1,0,2:T(8,128)(2,1)} collective-permute-done((bf16[8,128,512]{1,0,2:T(8,128)(2,1)}, bf16[8,128,512]{1,0,2:T(8,128)(2,1)}, u32[]{:S(2)}, u32[]{:S(2)}) %collective-permute-start.3) | collective-permute-done | bytes 1048608 | tf_op jit(solution)/shard_map/ppermute | solution.py:23
  147.5 1.6 pad_maximum_fusion
  149.1 1.9 %reverse_select_fusion = bf16[2,8,128,512]{2,1,0,3:T(8,128)(2,1)} fusion(bf16[2,8,128,512]{2,1,0,3:T(8,128)(2,1)S(1)} %pad_maximum_fusion, pred[]{:T(512)S(6)} %eq.44), kind=kLoop, calls=%fused_computation.5 | loop fusion | flops 1048576 | bytes 4194305 | tf_op jit(solution)/shard_map/jit(_where)/select_n | solution.py:27
  151.0 4.2 %squeeze.38 = bf16[2048,4,128]{0,2,1:T(8,128)(2,1)} reshape(bf16[2,8,128,512]{2,1,0,3:T(8,128)(2,1)} %reverse_select_fusion) | data formatting | bytes 4194304 | tf_op jit(solution)/shard_map/while/body/jit(dynamic_index_in_dim)/squeeze | solution.py:150
  155.2 2.5 %bitcast_reduce_fusion = (f32[128,4]{0,1:T(4,128)S(1)}, f32[4,2048,128]{2,1,0:T(8,128)S(1)}) fusion(bf16[2048,4,128]{0,2,1:T(8,128)(2,1)} %squeeze.38, bf16[16,4,8,128]{3,2,1,0:T(8,128)(2,1)S(1)} %fusion.13), kind=kOutput, calls=%fused_computation.1 | convolution fusion | flops 270532096 | bytes 6424576 | tf_op jit(solution)/shard_map/while/body/eval_jaxpr/thd,rhd->thr/dot_general | solution.py:117
  157.7 0.7 fusion.1
  158.4 1.2 copy-done.1
  159.7 4.0 %copy.38 = bf16[2048,512]{0,1:T(8,128)(2,1)} copy(bf16[2048,512]{1,0:T(8,128)(2,1)} %all-gather.8.cloned.1.call-done) | data formatting | bytes 4194304 | tf_op jit(solution)/shard_map/while/body/jit(dynamic_index_in_dim)/squeeze | solution.py:150
  163.6 4.0 %fusion.17 = bf16[128,4,128]{0,2,1:T(8,128)(2,1)S(1)} fusion(bf16[2048,4,128]{0,2,1:T(8,128)(2,1)} %bitcast.119, f32[4,2048,128]{2,1,0:T(8,128)} %copy-done.1, f32[128,4]{0,1:T(4,128)S(1)} %broadcast_maximum_fusion, f32[128,4]{0,1:T(4,128)S(1)} %get-tuple-element.48, f32[128,4]{0,1:T(4,128)S(1)} %get-tuple-element.47), kind=kOutput, calls=%fused_computation.23 | convolution fusion | flops 271777792 | bytes 6428672 | tf_op jit(solution)/shard_map/while/body/eval_jaxpr/thr,rhd->thd/dot_general | solution.py:124
  167.6 1.3 convolution_convert_fusion
  168.9 1.8 dynamic-slice_convert_fusion
  170.7 12.1 %reduce-scatter.2.cloned.1.call-done = bf16[128,1024]{1,0:T(8,128)(2,1)} async-done(((bf16[128,2048]{1,0:T(8,128)(2,1)}), bf16[128,1024]{1,0:T(8,128)(2,1)}) %reduce-scatter.2.cloned.1.call-update) | async-done | bytes 262160 | tf_op jit(solution)/shard_map/reduce_scatter | solution.py:156
  (26 shorter events, 0.2 us)
Async XLA Ops:
  7.2 160.5 %copy-start = (bf16[512,2048]{1,0:T(8,128)(2,1)S(1)}, bf16[512,2048]{1,0:T(8,128)(2,1)}, u32[]{:S(2)}) copy-start(bf16[512,2048]{1,0:T(8,128)(2,1)} %param.23) | copy-start | bytes 6291460
  7.2 9.9 %copy-start.5 = (bf16[64,2048]{1,0:T(8,128)(2,1)S(1)}, bf16[64,2048]{1,0:T(8,128)(2,1)}, u32[]{:S(2)}) copy-start(bf16[64,2048]{1,0:T(8,128)(2,1)} %param.14) | copy-start | bytes 786436
  7.2 47.5 %all-gather.10.cloned.1.call-start = ((), (), s32[]{:S(2)}) async-start(), calls=%async_computation.3 | async-start | bytes 3145728 | tf_op jit(solution)/shard_map/all_gather | solution.py:34
  15.5 39.2 %copy-start.7 = (s32[128]{0:T(128)S(1)}, s32[128]{0:T(128)}, u32[]{:S(2)}) copy-start(s32[128]{0:T(128)} %param.17) | copy-start | bytes 1540
  18.7 141.0 %all-gather.8.cloned.1.call-start = ((), (), s32[]{:S(2)}) async-start(), calls=%async_computation.1 | async-start | bytes 2228224 | tf_op jit(solution)/shard_map/all_gather | solution.py:141
  54.7 2.9 %copy-start.6 = (f32[2048]{0:T(1024)S(1)}, f32[2048]{0:T(1024)}, u32[]{:S(2)}) copy-start(f32[2048]{0:T(1024)} %param.19) | copy-start | bytes 24580
  57.3 2.4 %copy-start.2 = (f32[128,2048]{1,0:T(8,128)}, f32[128,2048]{1,0:T(8,128)S(1)}, u32[]{:S(2)}) copy-start(f32[128,2048]{1,0:T(8,128)S(1)} %get-tuple-element.50) | copy-start | bytes 3145732
  57.3 2.0 %copy-start.4 = (bf16[2048,512]{1,0:T(8,128)(2,1)S(1)}, bf16[2048,512]{1,0:T(8,128)(2,1)}, u32[]{:S(2)}) copy-start(bf16[2048,512]{1,0:T(8,128)(2,1)} %param.21) | copy-start | bytes 6291460
  59.7 1.4 collective-permute-start
  61.2 8.4 %collective-permute-start.1 = (bf16[2,128,512]{2,1,0:T(8,128)(2,1)S(1)}, bf16[2,128,512]{2,1,0:T(8,128)(2,1)S(1)}, u32[]{:S(2)}, u32[]{:S(2)}) collective-permute-start(bf16[2,128,512]{2,1,0:T(8,128)(2,1)S(1)} %get-tuple-element.46), channel_id=1, source_target_pairs={{0,2},{1,3},{2,0},{3,1},{4,6},{5,7},{6,4},{7,5},{8,10},{9,11},{10,... | collective-permute-start | bytes 786440 | tf_op jit(solution)/shard_map/ppermute | solution.py:23
  65.5 117.3 %reduce-scatter.2.cloned.1.call-start = ((), (), s32[]{:S(2)}) async-start(), calls=%async_computation.2 | async-start | bytes 786432 | tf_op jit(solution)/shard_map/reduce_scatter | solution.py:156
  69.8 17.5 %collective-permute-start.2 = (bf16[4,128,512]{2,1,0:T(8,128)(2,1)S(1)}, bf16[4,128,512]{2,1,0:T(8,128)(2,1)}, u32[]{:S(2)}, u32[]{:S(2)}) collective-permute-start(bf16[4,128,512]{2,1,0:T(8,128)(2,1)S(1)} %bitcast.120), channel_id=1, source_target_pairs={{0,4},{1,5},{2,6},{3,7},{4,0},{5,1},{6,2},{7,3},{8,12},{9,13},{10,... | collective-permute-start | bytes 1572872 | tf_op jit(solution)/shard_map/ppermute | solution.py:23
  92.1 55.4 %collective-permute-start.3 = (bf16[8,128,512]{1,0,2:T(8,128)(2,1)}, bf16[8,128,512]{1,0,2:T(8,128)(2,1)}, u32[]{:S(2)}, u32[]{:S(2)}) collective-permute-start(bf16[8,128,512]{1,0,2:T(8,128)(2,1)} %bitcast.117), channel_id=1, source_target_pairs={{0,8},{1,9},{2,10},{3,11},{4,12},{5,13},{6,14},{7,15},{8,0},{9,1},... | collective-permute-start | bytes 3145736 | tf_op jit(solution)/shard_map/ppermute | solution.py:23
  94.5 53.0 %copy-start.3 = (bf16[2,4,128,512]{2,1,0,3:T(4,128)(2,1)S(1)}, bf16[2,4,128,512]{2,1,0,3:T(4,128)(2,1)}, u32[]{:S(2)}) copy-start(bf16[2,4,128,512]{2,1,0,3:T(4,128)(2,1)} %copy.27) | copy-start | bytes 3145732
  157.7 1.9 %copy-start.1 = (f32[4,2048,128]{2,1,0:T(8,128)}, f32[4,2048,128]{2,1,0:T(8,128)S(1)}, u32[]{:S(2)}) copy-start(f32[4,2048,128]{2,1,0:T(8,128)S(1)} %get-tuple-element.52) | copy-start | bytes 12582916
Sparse Core Ops, SparseCore 0:
  18.8 35.7 all-gather.9
  65.6 65.0 all-gather.7
  169.0 13.7 reduce-scatter.1
